TPU v7x, 256 devices: a whole 4x4x8 slice. The times are simulated.
256 devices in a mesh: row: 8 (over z), col: 4 (over x_hi, core), chan: 8 (over x_lo, y).
Axes of the slice: x: 4 (x_hi: 2, x_lo: 2; x = x_hi * 2 + x_lo), y: 4, z: 8, core: 2. Of those that a mesh axis runs over, the one named last changes fastest.
Arguments:
- alignment_features: bfloat16 [2048, 512, 64], P('col', 'row'), may hold values from -8 to 8
- alignment_row_mask: int32 [2048], P('col'), may hold values 0 or 1
- residue_token_mask: int32 [512], P('row'), may hold values 0 or 1
- layer_norm_gain: float32 [64], replicated, may hold values from 0.25 to 1.75
- layer_norm_bias: float32 [64], replicated, may hold values from -3 to 3
- left_factor_weight: bfloat16 [64, 32], P(None, 'chan'), may hold values from -0.75 to 0.75
- right_factor_weight: bfloat16 [64, 32], replicated, may hold values from -0.75 to 0.75
- output_weight: bfloat16 [1024, 128], P('chan'), may hold values from -0.1875 to 0.1875
- output_bias: float32 [128], replicated, may hold values from -3 to 3
Outputs:
- pair_update: bfloat16 [512, 512, 128], P('col', ('row', 'chan'))
All inputs are finite; a program needn't handle non-finite values. No bound on the sum of `alignment_row_mask` or of `residue_token_mask` on one device may be relied on, other than what follows from the above.
Results may differ from a plain program's by a relative error of at most 0.0038.
Values may be sent and summed in bfloat16 or wider, within the bound.
No kernel may reach another device: no remote copies, remote signals or barrier semaphores. Data moves between devices by JAX's collectives and lax.ppermute only.
A program may use at most 128 MiB of HBM per device.

v0:
```python
import jax
import jax.numpy as jnp
from jax import lax
from jax.sharding import PartitionSpec as P


def apply_layer_norm(features, layer_norm_gain, layer_norm_bias):
    values = features.astype(jnp.float32)
    center = values - jnp.mean(values, axis=-1, keepdims=True)
    spread = jnp.mean(center * center, axis=-1, keepdims=True)
    return (center * lax.rsqrt(spread + 1e-05) * layer_norm_gain + layer_norm_bias).astype(
        jnp.bfloat16
    )


def make_factors(
    features,
    rows_used,
    tokens_used,
    layer_norm_gain,
    layer_norm_bias,
    left_factor_weight,
    right_factor_weight,
):
    normalized_features = apply_layer_norm(features, layer_norm_gain, layer_norm_bias)
    weight = rows_used[:, None].astype(jnp.float32) * tokens_used[None, :].astype(jnp.float32)
    left_part = (
        jnp.einsum(
            "stm,mc->sct",
            normalized_features,
            left_factor_weight,
            preferred_element_type=jnp.float32,
        )
        * weight[:, None, :]
    )
    right_part = (
        jnp.einsum(
            "stm,me->ste",
            normalized_features,
            right_factor_weight,
            preferred_element_type=jnp.float32,
        )
        * weight[:, :, None]
    )
    return (left_part.astype(jnp.bfloat16), right_part.astype(jnp.bfloat16))


def body(
    alignment_features,
    alignment_row_mask,
    residue_token_mask,
    layer_norm_gain,
    layer_norm_bias,
    left_factor_weight,
    right_factor_weight,
    output_weight,
    output_bias,
):
    every_feature, every_row = (
        lax.all_gather(alignment_features, "col", axis=0, tiled=True),
        lax.all_gather(alignment_row_mask, "col", axis=0, tiled=True),
    )
    left_part, right_every = make_factors(
        every_feature,
        every_row,
        residue_token_mask,
        layer_norm_gain,
        layer_norm_bias,
        left_factor_weight,
        right_factor_weight,
    )
    tokens_here = residue_token_mask.shape[0]
    mask_shaped = residue_token_mask.reshape(1, 1, tokens_here)
    owner_count = lax.axis_size("row") // lax.axis_size("col")
    block_tokens = tokens_here * owner_count
    col_index = lax.axis_index("col")
    left_every, mask_every = (
        lax.all_gather(left_part, "row", axis=2, tiled=True),
        lax.all_gather(mask_shaped, "row", axis=2, tiled=True),
    )
    left_block = lax.dynamic_slice_in_dim(left_every, col_index * block_tokens, block_tokens, 2)
    mask_block = lax.dynamic_slice_in_dim(mask_every, col_index * block_tokens, block_tokens, 2)
    products = jnp.einsum(
        "sci,sje->ijce", left_block, right_every, preferred_element_type=jnp.float32
    ).astype(jnp.bfloat16)
    flat_products = products.reshape(block_tokens * tokens_here, -1)
    partial_pairs = jnp.dot(
        flat_products, output_weight, preferred_element_type=jnp.float32
    ).reshape(block_tokens, tokens_here, -1)
    chan_count = lax.axis_size("chan")
    share = tokens_here // chan_count
    chan_index = lax.axis_index("chan")
    total_pairs = lax.psum(partial_pairs, "chan")
    summed = lax.dynamic_slice_in_dim(total_pairs, chan_index * share, share, 1)
    row_total = jnp.sum(every_row).astype(jnp.float32)
    first_used = mask_block.reshape(block_tokens).astype(jnp.float32)
    second_used = lax.dynamic_slice_in_dim(residue_token_mask, chan_index * share, share, 0).astype(
        jnp.float32
    )
    count = jnp.maximum(row_total * first_used[:, None] * second_used[None, :], 1.0)
    return ((summed + output_bias) / count[:, :, None]).astype(jnp.bfloat16)


def solution(mesh):
    in_specs = (
        P("col", "row", None),
        P("col"),
        P("row"),
        P(),
        P(),
        P(None, "chan"),
        P(),
        P("chan", None),
        P(),
    )
    out_specs = P("col", ("row", "chan"), None)
    return jax.shard_map(body, mesh=mesh, in_specs=in_specs, out_specs=out_specs, check_vma=False)
```

profile of v0, /device:TPU:1, one launch (start us, length us, event | category | flops | bytes accessed | tf_op | source)
XLA Modules:
  0.0 390.0 jit_solution(13971857495411139468)
XLA Ops:
  6.5 0.0 copy-start
  6.5 0.0 all-gather.5.cloned.1.call-start
  6.5 0.7 all-gather.5.cloned.1.call-update
  7.3 0.0 all-gather.7.cloned.1.call-start
  7.3 0.7 convert_element_type.49
  8.0 9.9 %all-gather.1 = s32[4,1,512]{2,1,0:T(1,128)S(1)} all-gather(s32[1,1,512]{2,1,0:T(1,128)} %bitcast.35), channel_id=1, replica_groups=mesh['row'=8,'col'=4,'chan'=8] {'col'}, dimensions={0}, use_global_device_ids=true | all-gather | bytes 10240 | tf_op jit(solution)/shard_map/all_gather | solution.py:61
  17.8 0.6 fusion.25
  18.5 0.1 broadcast_multiply_fusion
  18.6 0.0 copy-start.4
  18.6 0.0 copy-start.5
  18.6 107.3 %all-gather.5.cloned.1.call-done = bf16[2048,64,64]{0,2,1:T(8,128)(2,1)} async-done(((bf16[512,64,64]{0,2,1:T(8,128)(2,1)}), bf16[2048,64,64]{0,2,1:T(8,128)(2,1)}) %all-gather.5.cloned.1.call-update) | async-done | bytes 16777232 | tf_op jit(solution)/shard_map/all_gather | solution.py:60
  125.9 0.0 copy-start.1
  125.9 7.4 %convert_reduce_fusion = f32[2048,64]{0,1:T(8,128)S(1)} fusion(bf16[2048,64,64]{0,2,1:T(8,128)(2,1)} %all-gather.5.cloned.1.call-done), kind=kLoop, calls=%fused_computation.1 | loop fusion | flops 16646144 | bytes 17301504 | tf_op jit(solution)/shard_map/reduce_sum | solution.py:9
  133.3 3.2 copy-done.1
  136.5 5.4 %fusion.2 = f32[2048,64]{0,1:T(8,128)S(1)} fusion(bf16[2048,64,64]{0,2,1:T(8,128)(2,1)S(1)} %copy-done.1, f32[2048,64]{0,1:T(8,128)S(1)} %broadcast_multiply_fusion.1), kind=kLoop, calls=%fused_computation.4 | loop fusion | flops 33423360 | bytes 17825792 | tf_op jit(solution)/shard_map/reduce_sum | solution.py:10
  141.9 0.1 add_rsqrt_fusion
  142.0 0.0 copy-done.4
  142.0 0.0 copy-done.5
  142.0 0.0 copy-start.3
  142.0 6.6 %fusion.5 = bf16[2048,64,64]{0,2,1:T(8,128)(2,1)S(1)} fusion(bf16[2048,64,64]{0,2,1:T(8,128)(2,1)S(1)} %copy-done.1, f32[64]{0:T(128)S(1)} %copy-done.4, f32[64]{0:T(128)S(1)} %copy-done.5, f32[2048,64]{0,1:T(8,128)S(1)} %add_rsqrt_fusion, f32[2048,64]{0,1:T(8,128)S(1)} %broadcast_multiply_fusion.1), kind=kLoop, calls=%fused_computation.7 | loop fusion | flops 50331648 | bytes 34603520 | tf_op jit(solution)/shard_map/convert_element_type | solution.py:11
  148.7 0.0 copy-start.2
  148.7 5.7 %copy-done.2 = bf16[2048,64,64]{0,2,1:T(8,128)(2,1)} copy-done((bf16[2048,64,64]{0,2,1:T(8,128)(2,1)}, bf16[2048,64,64]{0,2,1:T(8,128)(2,1)S(1)}, u32[]{:S(2)}) %copy-start.2) | copy-done | bytes 16777240
  154.4 0.0 copy-done.3
  154.4 0.0 copy-start.7
  154.4 5.2 %fusion.13 = bf16[2048,4,64]{0,1,2:T(4,128)(2,1)} fusion(bf16[2048,64,64]{0,2,1:T(8,128)(2,1)S(1)} %fusion.5, f32[2048,64]{0,1:T(8,128)S(1)} %broadcast_multiply_fusion, bf16[64,4]{0,1:T(4,128)(2,1)S(1)} %copy-done.3), kind=kOutput, calls=%fused_computation.15 | convolution fusion | flops 68157440 | bytes 18350592 | tf_op jit(solution)/shard_map/stm,mc->sct/dot_general | solution.py:28
  159.6 0.0 all-gather.7.cloned.1.call-update
  159.6 0.0 all-reduce.3.cloned.1.call-start
  159.7 93.1 %all-gather.7.cloned.1.call-done = bf16[2048,4,512]{0,1,2:T(4,128)(2,1)} async-done(((bf16[2048,4,64]{0,1,2:T(4,128)(2,1)}), bf16[2048,4,512]{0,1,2:T(4,128)(2,1)}) %all-gather.7.cloned.1.call-update) | async-done | bytes 8388624 | tf_op jit(solution)/shard_map/all_gather | solution.py:78
  252.7 2.6 constant_dynamic-slice_fusion
  255.3 3.0 copy.18
  258.4 0.0 copy-done.7
  258.4 0.0 copy-start.9
  258.4 11.0 %fusion.15 = bf16[64,32,4,128]{3,1,2,0:T(8,128)(2,1)S(1)} fusion(bf16[2048,4,128]{2,0,1:T(8,128)(2,1)} %copy.18, f32[2048,64]{0,1:T(8,128)S(1)} %broadcast_multiply_fusion, bf16[2048,64,64]{0,2,1:T(8,128)(2,1)} %copy-done.2, bf16[64,32]{0,1:T(8,128)(2,1)S(1)} %copy-done.7), kind=kOutput, calls=%fused_computation.17 | convolution fusion | flops 4841275392 | bytes 21499904 | tf_op jit(solution)/shard_map/sci,sje->ijce/dot_general | solution.py:83
  269.4 0.0 copy-done
  269.4 2.7 fusion.20
  272.2 0.0 all-reduce.3.cloned.1.call-update
  272.8 0.0 copy-done.9
  272.9 0.6 dynamic-slice.1
  274.1 0.0 copy-done.8
  274.1 0.2 dynamic-update-slice
  274.4 9.1 %all-reduce = s32[512]{0:T(512)S(1)} all-reduce(s32[512]{0:T(512)S(1)} %dynamic-update-slice), channel_id=2, replica_groups=mesh['row'=8,'col'=4,'chan'=8] {'row'}, use_global_device_ids=true, to_apply=%add | all-reduce | flops 512 | bytes 4096
  283.5 0.1 dynamic-slice_convert_fusion
  283.5 0.1 convert_multiply_fusion
  283.6 0.1 multiply_maximum_fusion
  283.7 97.7 %all-reduce.3.cloned.1.call-done = f32[128,64,128]{2,0,1:T(8,128)} async-done(((f32[128,64,128]{2,0,1:T(8,128)}), f32[128,64,128]{2,0,1:T(8,128)}) %all-reduce.3.cloned.1.call-update) | async-done | bytes 4194320 | tf_op jit(solution)/shard_map/psum | solution.py:93
  381.3 0.0 copy-done.6
  381.3 1.2 divide_convert_fusion
  382.6 0.9 copy.15
  (4 shorter events, 0.0 us)
Async XLA Ops:
  6.5 262.9 %copy-start = (bf16[128,128]{1,0:T(8,128)(2,1)S(1)}, bf16[128,128]{1,0:T(8,128)(2,1)}, u32[]{:S(2)}) copy-start(bf16[128,128]{1,0:T(8,128)(2,1)} %param.16) | copy-start | bytes 98308
  6.5 119.3 %all-gather.5.cloned.1.call-start = ((), (), s32[]{:S(2)}) async-start(), calls=%async_computation | async-start | bytes 20971520 | tf_op jit(solution)/shard_map/all_gather | solution.py:60
  7.3 245.5 %all-gather.7.cloned.1.call-start = ((), (), s32[]{:S(2)}) async-start(), calls=%async_computation.1 | async-start | bytes 9437184 | tf_op jit(solution)/shard_map/all_gather | solution.py:78
  18.6 123.4 %copy-start.4 = (f32[64]{0:T(128)S(1)}, f32[64]{0:T(128)}, u32[]{:S(2)}) copy-start(f32[64]{0:T(128)} %param.13) | copy-start | bytes 772
  18.6 123.4 %copy-start.5 = (f32[64]{0:T(128)S(1)}, f32[64]{0:T(128)}, u32[]{:S(2)}) copy-start(f32[64]{0:T(128)} %param.12) | copy-start | bytes 772
  125.9 10.7 %copy-start.1 = (bf16[2048,64,64]{0,2,1:T(8,128)(2,1)S(1)}, bf16[2048,64,64]{0,2,1:T(8,128)(2,1)}, u32[]{:S(2)}) copy-start(bf16[2048,64,64]{0,2,1:T(8,128)(2,1)} %all-gather.5.cloned.1.call-done) | copy-start | bytes 50331652
  142.0 12.4 %copy-start.3 = (bf16[64,4]{0,1:T(4,128)(2,1)S(1)}, bf16[64,4]{0,1:T(4,128)(2,1)}, u32[]{:S(2)}) copy-start(bf16[64,4]{0,1:T(4,128)(2,1)} %param.14) | copy-start | bytes 1540
  148.7 5.7 %copy-start.2 = (bf16[2048,64,64]{0,2,1:T(8,128)(2,1)}, bf16[2048,64,64]{0,2,1:T(8,128)(2,1)S(1)}, u32[]{:S(2)}) copy-start(bf16[2048,64,64]{0,2,1:T(8,128)(2,1)S(1)} %fusion.5) | copy-start | bytes 50331652
  154.4 104.0 %copy-start.7 = (bf16[64,32]{0,1:T(8,128)(2,1)S(1)}, bf16[64,32]{0,1:T(8,128)(2,1)}, u32[]{:S(2)}) copy-start(bf16[64,32]{0,1:T(8,128)(2,1)} %param.15) | copy-start | bytes 12292
  159.6 221.7 %all-reduce.3.cloned.1.call-start = ((), (), s32[]{:S(2)}) async-start(), calls=%async_computation.2 | async-start | bytes 8388608 | tf_op jit(solution)/shard_map/psum | solution.py:93
  258.4 14.5 %copy-start.9 = (u32[256]{0:T(256)S(1)}, u32[256]{0:T(256)}, u32[]{:S(2)}) copy-start(u32[256]{0:T(256)} %constant.32) | copy-start | bytes 3076
  258.4 15.7 %copy-start.8 = (s32[64]{0:T(128)S(1)}, s32[64]{0:T(128)}, u32[]{:S(2)}) copy-start(s32[64]{0:T(128)} %param.11) | copy-start | bytes 772
  258.4 123.0 %copy-start.6 = (f32[128]{0:T(128)S(1)}, f32[128]{0:T(128)}, u32[]{:S(2)}) copy-start(f32[128]{0:T(128)} %param.17) | copy-start | bytes 1540
Sparse Core Ops, SparseCore 0:
  9.1 116.6 all-gather.4
  159.7 92.9 all-gather.6
  272.3 108.9 all-reduce.2
where the time goes:
time: 390 us
  waiting for transfers between devices  299 us (77%)
  other arithmetic  22.4 us (6%)
  blocking collectives  19 us (5%)
  matrix products  19 us (5%)
  local copies, waits for them, and re-layouts  16.3 us (4%)
  between operations  14.6 us (4%)
    all_gather x1, waiting for transfers between devices, body(): lax.all_gather(alignment_features, 'col', axis=0, tiled=True)  107 us
    psum x1, waiting for transfers between devices, body(): total_pairs = lax.psum(partial_pairs, 'chan')  97.7 us
    all_gather x1, waiting for transfers between devices, body(): lax.all_gather(left_part, 'row', axis=2, tiled=True)  93.1 us
    unnamed x24, local copies, waits for them, and re-layouts  12.8 us
    dot_general x1, matrix products, body(): jnp.einsum('sci,sje->ijce', left_block, right_every, preferred_element_ty...  11 us
    all_gather x1, blocking collectives, body(): lax.all_gather(alignment_row_mask, 'col', axis=0, tiled=True)  9.85 us
    unnamed x1, blocking collectives  9.1 us
  transfers between devices with their start and end apart: 3, of which 3 were waited for; matrix products, arithmetic and copies ran while one was open for 1% of the time, Pallas kernels for 0%

commit v1 on v0

--- a/solution.py
+++ b/solution.py
@@ -2,6 +2,11 @@
 import jax.numpy as jnp
 from jax import lax
 from jax.sharding import PartitionSpec as P
+
+
+def all_by_exchange(shard, name, d):
+    repeated = jnp.stack([shard] * lax.axis_size(name))
+    return jnp.concatenate(lax.all_to_all(repeated, name, 0, 0), axis=d)
 
 
 def apply_layer_norm(features, layer_norm_gain, layer_norm_bias):
@@ -75,7 +80,7 @@
     block_tokens = tokens_here * owner_count
     col_index = lax.axis_index("col")
     left_every, mask_every = (
-        lax.all_gather(left_part, "row", axis=2, tiled=True),
+        all_by_exchange(left_part, "row", 2),
         lax.all_gather(mask_shaped, "row", axis=2, tiled=True),
     )
     left_block = lax.dynamic_slice_in_dim(left_every, col_index * block_tokens, block_tokens, 2)

time: 390 us -> 493 us (1.26)
  waiting for transfers between devices: 299 us -> 390 us
  local copies, waits for them, and re-layouts: 16.3 us -> 23.8 us
  starting transfers between devices: 0.08 us -> 6.9 us
    all_to_all x0 -> x1, waiting for transfers between devices: none -> 187 us  [all_by_exchange(): return jnp.concatenate(lax.all_to_all(repeated, name, 0, 0), axis=d)]
    all_gather x1 -> x0, waiting for transfers between devices: 93.1 us -> none  [body(): lax.all_gather(left_part, 'row', axis=2, tiled=True)]
    all_to_all x0 -> x1, local copies, waits for them, and re-layouts: none -> 8.25 us  [all_by_exchange(): return jnp.concatenate(lax.all_to_all(repeated, name, 0, 0), axis=d)]
    all_to_all x0 -> x1, starting transfers between devices: none -> 6.86 us  [all_by_exchange(): return jnp.concatenate(lax.all_to_all(repeated, name, 0, 0), axis=d)]
    unnamed x24 -> x23, local copies, waits for them, and re-layouts: 12.8 us -> 9.85 us
  transfers between devices with their start and end apart: 3 -> 3, of which waited for: 3 -> 3; matrix products, arithmetic and copies ran while one was open for 1% -> 0% of each run, Pallas kernels for 0% -> 0%
where the time goes in v1:
time: 493 us
  waiting for transfers between devices  390 us (79%)
  local copies, waits for them, and re-layouts  23.8 us (5%)
  other arithmetic  22.4 us (5%)
  matrix products  18.1 us (4%)
  blocking collectives  16.9 us (3%)
  between operations  14.9 us (3%)
  starting transfers between devices  6.9 us (1%)
    all_to_all x1, waiting for transfers between devices, all_by_exchange(): return jnp.concatenate(lax.all_to_all(repeated, name, 0, 0), axis=d)  187 us
    all_gather x1, waiting for transfers between devices, body(): lax.all_gather(alignment_features, 'col', axis=0, tiled=True)  107 us
    psum x1, waiting for transfers between devices, body(): total_pairs = lax.psum(partial_pairs, 'chan')  95.1 us
    dot_general x1, matrix products, body(): jnp.einsum('sci,sje->ijce', left_block, right_every, preferred_element_ty...  11.1 us
  transfers between devices with their start and end apart: 3, of which 3 were waited for; matrix products, arithmetic and copies ran while one was open for 0% of the time, Pallas kernels for 0%

profile of v1, /device:TPU:1, one launch (start us, length us, event | category | flops | bytes accessed | tf_op | source)
XLA Modules:
  0.0 493.2 jit_solution(15239559342583486077)
XLA Ops:
  6.5 0.0 copy-start
  6.5 0.0 all-gather.4.cloned.1.call-start
  6.5 0.7 all-gather.4.cloned.1.call-update
  7.3 0.7 convert_element_type.49
  7.9 9.8 %all-gather.1 = s32[4,1,512]{2,1,0:T(1,128)S(1)} all-gather(s32[1,1,512]{2,1,0:T(1,128)} %bitcast.40), channel_id=1, replica_groups=mesh['row'=8,'col'=4,'chan'=8] {'col'}, dimensions={0}, use_global_device_ids=true | all-gather | bytes 10240 | tf_op jit(solution)/shard_map/all_gather | solution.py:66
  17.8 0.6 fusion.27
  18.4 0.1 broadcast_multiply_fusion
  18.5 0.0 copy-start.4
  18.5 0.0 copy-start.5
  18.5 107.3 %all-gather.4.cloned.1.call-done = bf16[2048,64,64]{0,2,1:T(8,128)(2,1)} async-done(((bf16[512,64,64]{0,2,1:T(8,128)(2,1)}), bf16[2048,64,64]{0,2,1:T(8,128)(2,1)}) %all-gather.4.cloned.1.call-update) | async-done | bytes 16777232 | tf_op jit(solution)/shard_map/all_gather | solution.py:65
  125.9 0.0 copy-start.1
  125.9 7.3 %convert_reduce_fusion = f32[2048,64]{0,1:T(8,128)S(1)} fusion(bf16[2048,64,64]{0,2,1:T(8,128)(2,1)} %all-gather.4.cloned.1.call-done), kind=kLoop, calls=%fused_computation.1 | loop fusion | flops 16646144 | bytes 17301504 | tf_op jit(solution)/shard_map/reduce_sum | solution.py:14
  133.3 3.3 copy-done.1
  136.5 5.4 %fusion.2 = f32[2048,64]{0,1:T(8,128)S(1)} fusion(bf16[2048,64,64]{0,2,1:T(8,128)(2,1)S(1)} %copy-done.1, f32[2048,64]{0,1:T(8,128)S(1)} %broadcast_multiply_fusion.1), kind=kLoop, calls=%fused_computation.4 | loop fusion | flops 33423360 | bytes 17825792 | tf_op jit(solution)/shard_map/reduce_sum | solution.py:15
  141.9 0.1 add_rsqrt_fusion
  142.0 0.0 copy-done.4
  142.0 0.0 copy-done.5
  142.0 0.0 copy-start.3
  142.0 6.6 %fusion.5 = bf16[2048,64,64]{0,2,1:T(8,128)(2,1)S(1)} fusion(bf16[2048,64,64]{0,2,1:T(8,128)(2,1)S(1)} %copy-done.1, f32[64]{0:T(128)S(1)} %copy-done.4, f32[64]{0:T(128)S(1)} %copy-done.5, f32[2048,64]{0,1:T(8,128)S(1)} %add_rsqrt_fusion, f32[2048,64]{0,1:T(8,128)S(1)} %broadcast_multiply_fusion.1), kind=kLoop, calls=%fused_computation.7 | loop fusion | flops 50331648 | bytes 34603520 | tf_op jit(solution)/shard_map/convert_element_type | solution.py:16
  148.7 0.0 copy-start.2
  148.7 5.7 %copy-done.2 = bf16[2048,64,64]{0,2,1:T(8,128)(2,1)} copy-done((bf16[2048,64,64]{0,2,1:T(8,128)(2,1)}, bf16[2048,64,64]{0,2,1:T(8,128)(2,1)S(1)}, u32[]{:S(2)}) %copy-start.2) | copy-done | bytes 16777240
  154.4 0.0 copy-done.3
  154.4 4.4 fusion.13
  158.8 0.6 copy.17
  159.3 4.3 stack.2
  163.6 0.0 copy-start.7
  163.6 6.9 %all-to-all-start = ((bf16[8,2048,4,64]{1,3,2,0:T(8,128)(2,1)}), bf16[8,2048,4,64]{1,3,2,0:T(8,128)(2,1)}, u32[]{:S(2)}, u32[]{:S(2)}) async-start(bf16[8,2048,4,64]{1,3,2,0:T(8,128)(2,1)} %stack.2), calls=%async_computation | async-start | bytes 16777216 | tf_op jit(solution)/shard_map/all_to_all | solution.py:9
  170.5 0.0 all-reduce.3.cloned.1.call-start
  170.5 187.0 %all-to-all-done = bf16[8,2048,4,64]{1,3,2,0:T(8,128)(2,1)} async-done(((bf16[8,2048,4,64]{1,3,2,0:T(8,128)(2,1)}), bf16[8,2048,4,64]{1,3,2,0:T(8,128)(2,1)}, u32[]{:S(2)}, u32[]{:S(2)}) %all-to-all-start) | async-done | bytes 8388640 | tf_op jit(solution)/shard_map/all_to_all | solution.py:9
  357.6 8.2 %copy.18 = bf16[8,2048,4,64]{1,3,0,2:T(8,128)(2,1)} copy(bf16[8,2048,4,64]{1,3,2,0:T(8,128)(2,1)} %all-to-all-done) | data formatting | bytes 16777216 | tf_op jit(solution)/shard_map/all_to_all | solution.py:9
  365.8 0.0 copy-done.7
  365.8 0.0 copy-start.9
  365.8 11.1 %fusion.16 = bf16[64,32,4,128]{3,1,2,0:T(8,128)(2,1)S(1)} fusion(bf16[2048,4,512]{0,2,1:T(8,128)(2,1)} %bitcast.37, s32[]{:T(128)S(6)} %select_n.8, f32[2048,64]{0,1:T(8,128)S(1)} %broadcast_multiply_fusion, bf16[2048,64,64]{0,2,1:T(8,128)(2,1)} %copy-done.2, bf16[64,32]{0,1:T(8,128)(2,1)S(1)} %copy-done.7), kind=kOutput, calls=%fused_computation.18 | convolution fusion | flops 4841275392 | bytes 21499908 | tf_op jit(solution)/shard_map/sci,sje->ijce/dot_general | solution.py:88
  376.9 0.0 copy-done
  376.9 2.7 fusion.21
  379.6 0.0 all-reduce.3.cloned.1.call-update
  380.3 0.0 copy-done.9
  380.3 0.6 dynamic-slice.1
  381.5 0.0 copy-done.8
  381.6 0.2 dynamic-update-slice
  381.8 7.0 %all-reduce = s32[512]{0:T(512)S(1)} all-reduce(s32[512]{0:T(512)S(1)} %dynamic-update-slice), channel_id=2, replica_groups=mesh['row'=8,'col'=4,'chan'=8] {'row'}, use_global_device_ids=true, to_apply=%add | all-reduce | flops 512 | bytes 4096
  388.8 0.1 dynamic-slice_convert_fusion
  388.9 0.1 convert_multiply_fusion
  389.0 0.1 multiply_maximum_fusion
  389.0 95.1 %all-reduce.3.cloned.1.call-done = f32[128,64,128]{2,0,1:T(8,128)} async-done(((f32[128,64,128]{2,0,1:T(8,128)}), f32[128,64,128]{2,0,1:T(8,128)}) %all-reduce.3.cloned.1.call-update) | async-done | bytes 4194320 | tf_op jit(solution)/shard_map/psum | solution.py:98
  484.2 0.0 copy-done.6
  484.2 1.2 divide_convert_fusion
  485.4 0.9 copy.21
  (4 shorter events, 0.0 us)
Async XLA Ops:
  6.5 370.4 %copy-start = (bf16[128,128]{1,0:T(8,128)(2,1)S(1)}, bf16[128,128]{1,0:T(8,128)(2,1)}, u32[]{:S(2)}) copy-start(bf16[128,128]{1,0:T(8,128)(2,1)} %param.16) | copy-start | bytes 98308
  6.5 119.3 %all-gather.4.cloned.1.call-start = ((), (), s32[]{:S(2)}) async-start(), calls=%async_computation.1 | async-start | bytes 20971520 | tf_op jit(solution)/shard_map/all_gather | solution.py:65
  18.5 123.5 %copy-start.4 = (f32[64]{0:T(128)S(1)}, f32[64]{0:T(128)}, u32[]{:S(2)}) copy-start(f32[64]{0:T(128)} %param.13) | copy-start | bytes 772
  18.5 123.5 %copy-start.5 = (f32[64]{0:T(128)S(1)}, f32[64]{0:T(128)}, u32[]{:S(2)}) copy-start(f32[64]{0:T(128)} %param.12) | copy-start | bytes 772
  125.9 10.7 %copy-start.1 = (bf16[2048,64,64]{0,2,1:T(8,128)(2,1)S(1)}, bf16[2048,64,64]{0,2,1:T(8,128)(2,1)}, u32[]{:S(2)}) copy-start(bf16[2048,64,64]{0,2,1:T(8,128)(2,1)} %all-gather.4.cloned.1.call-done) | copy-start | bytes 50331652
  142.0 12.4 %copy-start.3 = (bf16[64,4]{0,1:T(4,128)(2,1)S(1)}, bf16[64,4]{0,1:T(4,128)(2,1)}, u32[]{:S(2)}) copy-start(bf16[64,4]{0,1:T(4,128)(2,1)} %param.14) | copy-start | bytes 1540
  148.7 5.7 %copy-start.2 = (bf16[2048,64,64]{0,2,1:T(8,128)(2,1)}, bf16[2048,64,64]{0,2,1:T(8,128)(2,1)S(1)}, u32[]{:S(2)}) copy-start(bf16[2048,64,64]{0,2,1:T(8,128)(2,1)S(1)} %fusion.5) | copy-start | bytes 50331652
  163.6 202.2 %copy-start.7 = (bf16[64,32]{0,1:T(8,128)(2,1)S(1)}, bf16[64,32]{0,1:T(8,128)(2,1)}, u32[]{:S(2)}) copy-start(bf16[64,32]{0,1:T(8,128)(2,1)} %param.15) | copy-start | bytes 12292
  163.6 193.9 %all-to-all-start = ((bf16[8,2048,4,64]{1,3,2,0:T(8,128)(2,1)}), bf16[8,2048,4,64]{1,3,2,0:T(8,128)(2,1)}, u32[]{:S(2)}, u32[]{:S(2)}) async-start(bf16[8,2048,4,64]{1,3,2,0:T(8,128)(2,1)} %stack.2), calls=%async_computation | async-start | bytes 16777216 | tf_op jit(solution)/shard_map/all_to_all | solution.py:9
  170.5 313.7 %all-reduce.3.cloned.1.call-start = ((), (), s32[]{:S(2)}) async-start(), calls=%async_computation.2 | async-start | bytes 8388608 | tf_op jit(solution)/shard_map/psum | solution.py:98
  365.8 14.5 %copy-start.9 = (u32[256]{0:T(256)S(1)}, u32[256]{0:T(256)}, u32[]{:S(2)}) copy-start(u32[256]{0:T(256)} %constant.32) | copy-start | bytes 3076
  365.8 15.7 %copy-start.8 = (s32[64]{0:T(128)S(1)}, s32[64]{0:T(128)}, u32[]{:S(2)}) copy-start(s32[64]{0:T(128)} %param.11) | copy-start | bytes 772
  365.8 118.4 %copy-start.6 = (f32[128]{0:T(128)S(1)}, f32[128]{0:T(128)}, u32[]{:S(2)}) copy-start(f32[128]{0:T(128)} %param.17) | copy-start | bytes 1540
Sparse Core Ops, SparseCore 0:
  9.1 116.6 all-gather.3
  379.8 104.3 all-reduce.2
